TPU v7x, 256 devices: a whole 4x4x8 slice. The times are simulated.
256 devices in a mesh: dp: 128 (over y, z, x), rep: 2 (over core).
Axes of the slice: x: 4, y: 4, z: 8, core: 2. Of those that a mesh axis runs over, the one named last changes fastest.
Arguments:
- embeddings: float32 [131072, 1024], P(('dp', 'rep')), may hold values from -6 to 6
- cluster_ids: int32 [131072, 1], P(('dp', 'rep')), may hold values from 0 to 255; in each aligned block of 512 rows (0 to 511, 512 to 1023, ...) at most 4 rows name the same one
- boundary_slots: int32 [256, 2, 256], P(('dp', 'rep')), may hold values from 0 to 1023
Outputs:
- member_max: float32 [256, 1024], P(('dp', 'rep'))
- centrality: float32 [256, 1024], P(('dp', 'rep'))
Inputs may be any that keep to these rules, and one draw needn't show every extreme that they name: `cluster_ids`: among the rows of one device, at most 4 name the same cluster, a bound that some block reaches of them; every cluster is named by some row.
All inputs are finite; a program needn't handle non-finite values.
Results may differ from a plain program's by a relative error of at most 0.0024.
Values may be sent and summed in bfloat16 or wider, within the bound.
A program may use at most 64 MiB of HBM per device.

v0:
```python
import jax
import jax.numpy as jnp
from jax import lax
from jax.sharding import PartitionSpec as P

SLOTS = 1024
eps = 1e-06


def from_behind(array, axis, by):
    peers = lax.axis_size(axis)
    pairs = [(i, i + by) for i in range(peers) if 0 <= i + by < peers]
    return lax.ppermute(array, axis, pairs)


def per_device(embeddings, cluster_ids, boundary_slots):
    n_chips = lax.axis_size("dp")
    n_cores = lax.axis_size("rep")
    owners = n_chips * n_cores
    width = embeddings.shape[1]
    slots = SLOTS
    capacity = slots // owners
    bound = boundary_slots.shape[2]
    me = lax.axis_index(("dp", "rep"))
    labels = cluster_ids[:, 0]
    member_of = labels[:, None] == jnp.arange(owners, dtype=jnp.int32)[None, :]
    running = jnp.cumsum(member_of.astype(jnp.int32), axis=0)
    ranks = jnp.sum(jnp.where(member_of, running, 0), axis=1) - 1
    targets = labels * capacity + ranks
    unit_full = embeddings * lax.rsqrt(
        jnp.sum(embeddings * embeddings, axis=1, keepdims=True) + eps
    )
    unit_half = unit_full.astype(jnp.bfloat16)
    outgoing = jnp.zeros((slots, width), jnp.bfloat16).at[targets].set(unit_half)
    member_half = member_of.astype(jnp.bfloat16)
    shaped = outgoing.reshape(n_chips, n_cores, capacity, width)
    arrived = lax.all_to_all(
        lax.all_to_all(shaped, "dp", split_axis=0, concat_axis=0, tiled=True),
        "rep",
        split_axis=1,
        concat_axis=1,
        tiled=True,
    )
    members = arrived.reshape(slots, width)
    partial_sums = lax.dot_general(
        member_half, unit_half, (((0,), (0,)), ((), ())), preferred_element_type=jnp.float32
    )
    total = lax.psum(partial_sums, ("dp", "rep"))
    own_sum = lax.dynamic_slice_in_dim(total, me, 1, 0)
    direction = own_sum[0] * lax.rsqrt(jnp.sum(own_sum * own_sum) + eps)
    lengths = jnp.einsum("se,se->s", members, members, preferred_element_type=jnp.float32)
    filled = lengths > 0.5
    filled_int = filled.astype(jnp.int32)
    count = jnp.sum(filled_int)
    order = jnp.argsort(1 - filled_int, stable=True)
    picks = boundary_slots[0] % count
    positions = order[picks.reshape(-1)]
    outward = members[positions]
    lower = from_behind(outward[bound:], ("dp", "rep"), 1)
    upper = from_behind(outward[:bound], ("dp", "rep"), -1)
    candidates = jnp.concatenate([members, lower, upper], axis=0)
    cand_ok = jnp.concatenate(
        [filled, jnp.full((bound,), me > 0), jnp.full((bound,), me < owners - 1)]
    )
    column = jnp.arange(slots + 2 * bound, dtype=jnp.int32)
    block = min(512, slots)

    def one_block(start):
        block_rows = lax.dynamic_slice_in_dim(members, start, block, 0)
        scores = lax.dot_general(
            block_rows, candidates, (((1,), (1,)), ((), ())), preferred_element_type=jnp.float32
        )
        row_pos = start + jnp.arange(block, dtype=jnp.int32)
        keep = cand_ok[None, :] & (column[None, :] != row_pos[:, None])
        return jnp.max(jnp.where(keep, scores, -1.0), axis=1)

    starts = jnp.arange(slots // block, dtype=jnp.int32) * block
    best = lax.map(one_block, starts).reshape(slots)
    member_max = jnp.where(filled, best, 0.0)
    central = jnp.dot(
        members, direction, precision=lax.Precision.HIGHEST, preferred_element_type=jnp.float32
    )
    centrality = jnp.where(filled, central, 0.0)
    return (member_max[None, :], centrality[None, :])


def solution(mesh):
    placed = (P(("dp", "rep"), None), P(("dp", "rep"), None), P(("dp", "rep"), None, None))
    return jax.shard_map(
        per_device,
        mesh=mesh,
        in_specs=placed,
        out_specs=(P(("dp", "rep"), None), P(("dp", "rep"), None)),
        check_vma=False,
    )
```

profile of v0, /device:TPU:8, one launch (start us, length us, event | category | flops | bytes accessed | tf_op | source)
XLA Modules:
  0.0 374.8 jit_solution(14825172263603566123)
XLA Ops:
  7.2 0.0 copy-start.1
  7.2 1.8 multiply_reduce_fusion
  9.0 0.0 copy-start
  9.0 0.0 copy-done.1
  9.0 0.1 copy.12
  9.1 0.2 fusion.10
  9.4 0.1 copy.13
  9.5 0.2 fusion.9
  9.8 0.8 copy-done
  10.6 4.2 %scatter_custom_fusion = bf16[1024,1024]{1,0:T(8,128)(2,1)} fusion(s32[512]{0:T(512)S(1)} %bitcast.58, bf16[]{:T(256)} %constant.27.clone.1, f32[512,1024]{1,0:T(8,128)S(1)} %copy-done, f32[512]{0:T(512)S(1)} %add_rsqrt_fusion), kind=kCustom, calls=%fused_computation.16 | custom fusion | flops 1048576 | bytes 4196354 | tf_op jit(solution)/shard_map/scatter | solution.py:34
  14.7 4.1 %reshape.106 = bf16[128,2,4,1024]{3,2,1,0:T(4,128)(2,1)} reshape(bf16[1024,1024]{1,0:T(8,128)(2,1)} %scatter_custom_fusion) | data formatting | bytes 4194304 | tf_op jit(solution)/shard_map/reshape | solution.py:36
  18.8 15.9 %all-to-all-start = ((bf16[128,2,4,1024]{3,2,1,0:T(4,128)(2,1)}), bf16[128,2,4,1024]{3,2,1,0:T(4,128)(2,1)}, u32[]{:S(2)}, u32[]{:S(2)}) async-start(bf16[128,2,4,1024]{3,2,1,0:T(4,128)(2,1)} %reshape.106), calls=%async_computation | async-start | bytes 4194304 | tf_op jit(solution)/shard_map/all_to_all | solution.py:38
  34.8 0.0 all-reduce.2.cloned.1.call-start
  34.8 1.7 fusion.12
  36.5 0.0 all-reduce.2.cloned.1.call-update
  36.5 268.0 %all-reduce.2.cloned.1.call-done = f32[256,1024]{1,0:T(8,128)} async-done(((f32[256,1024]{1,0:T(8,128)}), f32[256,1024]{1,0:T(8,128)}) %all-reduce.2.cloned.1.call-update) | async-done | bytes 1048592 | tf_op jit(solution)/shard_map/psum | solution.py:48
  304.5 1.4 multiply_reduce_fusion.1
  306.6 0.0 all-to-all-done
  306.6 2.3 copy.14
  308.9 5.4 %all_to_all.10 = bf16[128,2,4,1024]{3,2,0,1:T(4,128)(2,1)S(1)} all-to-all(bf16[128,2,4,1024]{3,2,0,1:T(4,128)(2,1)S(1)} %copy.14), channel_id=1, replica_groups=mesh['dp'=128,'rep'=2] {'rep'}, dimensions={1} | all-to-all | bytes 4194304 | tf_op jit(solution)/shard_map/all_to_all | solution.py:37
  314.3 2.6 copy.15
  317.0 2.5 reshape.107
  319.5 0.0 copy-start.2
  319.5 0.5 fusion.6
  320.0 2.5 fusion.15
  322.5 0.6 broadcast_select_fusion
  323.1 0.6 convert_reduce_fusion
  325.0 0.0 copy-done.2
  325.0 0.1 remainder_bitcast_fusion
  325.2 4.4 %sort.17 = (s32[1024]{0:T(1024)}, s32[1024]{0:T(1024)S(1)}) sort(s32[1024]{0:T(1024)S(1)} %get-tuple-element.73, s32[1024]{0:T(1024)S(1)} %iota.25), dimensions={0}, to_apply=%region_5.6 | sort | flops 10240 | bytes 16384 | tf_op jit(solution)/shard_map/jit(argsort)/sort | solution.py:55
  329.6 2.3 gather_fusion
  331.9 2.1 gather_fusion.1
  334.0 1.1 fusion.21
  335.0 2.0 collective-permute-start
  337.1 7.7 %collective-permute-start.1 = (bf16[256,1024]{1,0:T(8,128)(2,1)}, bf16[256,1024]{1,0:T(8,128)(2,1)S(1)}, u32[]{:S(2)}, u32[]{:S(2)}) collective-permute-start(bf16[256,1024]{1,0:T(8,128)(2,1)} %get-tuple-element.71), channel_id=1, source_target_pairs={{1,0},{2,1},{3,2},{4,3},{5,4},{6,5},{7,6},{8,7},{9,8},{10,9},{11,1... | collective-permute-start | bytes 1572872 | tf_op jit(solution)/shard_map/ppermute | solution.py:13
  344.9 5.1 %collective-permute-done = bf16[256,1024]{1,0:T(8,128)(2,1)S(1)} collective-permute-done((bf16[256,1024]{1,0:T(8,128)(2,1)}, bf16[256,1024]{1,0:T(8,128)(2,1)S(1)}, u32[]{:S(2)}, u32[]{:S(2)}) %collective-permute-start) | collective-permute-done | bytes 524320 | tf_op jit(solution)/shard_map/ppermute | solution.py:13
  349.9 1.9 collective-permute-done.1
  351.8 1.9 pad_maximum_fusion
  353.7 13.6 %while.11 = (s32[]{:T(128)}, f32[2,512]{1,0:T(2,128)S(1)}, pred[1536]{0:T(1024)(128)(4,1)S(1)}, s32[2]{0:T(128)S(1)}, bf16[1024,1024]{1,0:T(8,128)(2,1)S(1)}, /*...) while((s32[]{:T(128)}, f32[2,512]{1,0:T(2,128)S(1)}, ...), condition=%wide.region_9.10_spmd.clone, body=%wide.region_7.9_spmd.clone.sunk | while | flops 1613758464 | bytes 4206743 | solution.py:78
  353.7 0.5 dynamic_slice.23
  355.9 0.5 iota_add_fusion.2
  356.4 4.0 %fusion.29 = f32[512]{0:T(512)S(1)} fusion(bf16[1536,1024]{1,0:T(8,128)(2,1)} %get-tuple-element.134, s32[512]{0:T(512)S(1)} %iota_add_fusion.2, pred[1536]{0:T(1024)(128)(4,1)S(1)} %get-tuple-element.131, bf16[1024,1024]{1,0:T(8,128)(2,1)S(1)} %get-tuple-element.133, s32[]{:T(128)S(6)} %select_n.90), kind=kOutput, calls=%fused_computation.7.clone.1 | convolution fusion | flops 1613757952 | bytes 4200452 | tf_op jit(solution)/shard_map/while/body/eval_jaxpr/dot_general | solution.py:70
  360.5 0.6 dynamic_slice.23
  362.7 0.5 iota_add_fusion.2
  363.2 4.0 %fusion.29 = f32[512]{0:T(512)S(1)} fusion(bf16[1536,1024]{1,0:T(8,128)(2,1)} %get-tuple-element.134, s32[512]{0:T(512)S(1)} %iota_add_fusion.2, pred[1536]{0:T(1024)(128)(4,1)S(1)} %get-tuple-element.131, bf16[1024,1024]{1,0:T(8,128)(2,1)S(1)} %get-tuple-element.133, s32[]{:T(128)S(6)} %select_n.90), kind=kOutput, calls=%fused_computation.7.clone.1 | convolution fusion | flops 1613757952 | bytes 4200452 | tf_op jit(solution)/shard_map/while/body/eval_jaxpr/dot_general | solution.py:70
  367.3 0.6 broadcast_select_fusion.1
  (22 shorter events, 0.2 us)
Async XLA Ops:
  7.2 1.8 copy-start.1
  9.0 1.6 copy-start
  18.8 287.7 %all-to-all-start = ((bf16[128,2,4,1024]{3,2,1,0:T(4,128)(2,1)}), bf16[128,2,4,1024]{3,2,1,0:T(4,128)(2,1)}, u32[]{:S(2)}, u32[]{:S(2)}) async-start(bf16[128,2,4,1024]{3,2,1,0:T(4,128)(2,1)} %reshape.106), calls=%async_computation | async-start | bytes 4194304 | tf_op jit(solution)/shard_map/all_to_all | solution.py:38
  34.8 269.8 %all-reduce.2.cloned.1.call-start = ((), (), s32[]{:S(2)}) async-start(), calls=%async_computation.2 | async-start | bytes 2097152 | tf_op jit(solution)/shard_map/psum | solution.py:48
  319.5 5.5 %copy-start.2 = (s32[1,2,256]{2,1,0:T(2,128)S(1)}, s32[1,2,256]{2,1,0:T(2,128)}, u32[]{:S(2)}) copy-start(s32[1,2,256]{2,1,0:T(2,128)} %param.7) | copy-start | bytes 6148
  335.0 14.9 %collective-permute-start = (bf16[256,1024]{1,0:T(8,128)(2,1)}, bf16[256,1024]{1,0:T(8,128)(2,1)S(1)}, u32[]{:S(2)}, u32[]{:S(2)}) collective-permute-start(bf16[256,1024]{1,0:T(8,128)(2,1)} %get-tuple-element.70), channel_id=1, source_target_pairs={{0,1},{1,2},{2,3},{3,4},{4,5},{5,6},{6,7},{7,8},{8,9},{9,10},{10,1... | collective-permute-start | bytes 1572872 | tf_op jit(solution)/shard_map/ppermute | solution.py:13
  337.1 14.7 %collective-permute-start.1 = (bf16[256,1024]{1,0:T(8,128)(2,1)}, bf16[256,1024]{1,0:T(8,128)(2,1)S(1)}, u32[]{:S(2)}, u32[]{:S(2)}) collective-permute-start(bf16[256,1024]{1,0:T(8,128)(2,1)} %get-tuple-element.71), channel_id=1, source_target_pairs={{1,0},{2,1},{3,2},{4,3},{5,4},{6,5},{7,6},{8,7},{9,8},{10,9},{11,1... | collective-permute-start | bytes 1572872 | tf_op jit(solution)/shard_map/ppermute | solution.py:13
Sparse Core Ops, SparseCore 0:
  41.0 263.4 all-reduce.1
where the time goes:
time: 376 us; the launch traced here: 375 us
  waiting for transfers between devices  275 us (73%)
  starting transfers between devices  25.7 us (7%)
  local copies, waits for them, and re-layouts  19.2 us (5%)
  other arithmetic  17.7 us (5%)
  between operations  16.3 us (4%)
  matrix products  12.1 us (3%)
  blocking collectives  5.42 us (1%)
    psum x1, waiting for transfers between devices, per_device(): total = lax.psum(partial_sums, ('dp', 'rep'))  268 us
    all_to_all x1, starting transfers between devices, per_device(): lax.all_to_all(shaped, 'dp', split_axis=0, concat_axis=0, tiled=True)  15.9 us
    ppermute x2, starting transfers between devices, from_behind(): return lax.ppermute(array, axis, pairs)  9.77 us
    dot_general x2, matrix products, one_block(): lax.dot_general(block_rows, candidates, (((1,), (1,)), ((), ())), preferr...  8.01 us
  transfers between devices with their start and end apart: 4, of which 3 were waited for; matrix products, arithmetic and copies ran while one was open for 1% of the time, Pallas kernels for 0%

commit v1 on v0

--- a/solution.py
+++ b/solution.py
@@ -34,12 +34,20 @@
     outgoing = jnp.zeros((slots, width), jnp.bfloat16).at[targets].set(unit_half)
     member_half = member_of.astype(jnp.bfloat16)
     shaped = outgoing.reshape(n_chips, n_cores, capacity, width)
-    arrived = lax.all_to_all(
-        lax.all_to_all(shaped, "dp", split_axis=0, concat_axis=0, tiled=True),
-        "rep",
-        split_axis=1,
-        concat_axis=1,
-        tiled=True,
+    arrived = jnp.concatenate(
+        lax.all_to_all(
+            jnp.stack(
+                jnp.split(
+                    lax.all_to_all(shaped, "dp", split_axis=0, concat_axis=0, tiled=True),
+                    lax.axis_size("rep"),
+                    axis=1,
+                )
+            ),
+            "rep",
+            0,
+            0,
+        ),
+        axis=1,
     )
     members = arrived.reshape(slots, width)
     partial_sums = lax.dot_general(

time: 376 us -> 377 us (level)
    all_to_all x2 -> x0, local copies, waits for them, and re-layouts: 4.94 us -> none  [the longest x1 2.63 us: per_device(): lax.all_to_all(lax.all_to_all(shaped, 'dp', split_axis=0, concat_axis=0,...]
    another operation x3 -> x5, local copies, waits for them, and re-layouts: 0.11 us -> 4.91 us  [the longest x1 2.54 us: per_device(): members = arrived.reshape(slots, width)]
where the time goes in v1:
time: 377 us; the launch traced here: 376 us
  waiting for transfers between devices  275 us (73%)
  starting transfers between devices  25.7 us (7%)
  local copies, waits for them, and re-layouts  19.2 us (5%)
  other arithmetic  19.2 us (5%)
  between operations  16.3 us (4%)
  matrix products  12.1 us (3%)
  blocking collectives  5.42 us (1%)
    psum x1, waiting for transfers between devices, per_device(): total = lax.psum(partial_sums, ('dp', 'rep'))  268 us
    all_to_all x1, starting transfers between devices, per_device(): lax.all_to_all(shaped, 'dp', split_axis=0, concat_axis=0, tiled=True)  15.9 us
    ppermute x2, starting transfers between devices, from_behind(): return lax.ppermute(array, axis, pairs)  9.77 us
    dot_general x2, matrix products, one_block(): lax.dot_general(block_rows, candidates, (((1,), (1,)), ((), ())), preferr...  8.01 us
  transfers between devices with their start and end apart: 4, of which 3 were waited for; matrix products, arithmetic and copies ran while one was open for 1% of the time, Pallas kernels for 0%

profile of v1, /device:TPU:8, one launch (start us, length us, event | category | flops | bytes accessed | tf_op | source)
XLA Modules:
  0.0 376.2 jit_solution(17758107287226644432)
XLA Ops:
  7.2 0.0 copy-start.1
  7.2 1.8 multiply_reduce_fusion
  9.0 0.0 copy-start
  9.0 0.0 copy-done.1
  9.0 0.1 copy.7
  9.1 0.2 fusion.10
  9.4 0.1 copy.8
  9.5 0.2 fusion.9
  9.8 0.8 copy-done
  10.6 4.2 %scatter_custom_fusion = bf16[1024,1024]{1,0:T(8,128)(2,1)} fusion(s32[512]{0:T(512)S(1)} %bitcast.68, bf16[]{:T(256)} %constant.27.clone.1, f32[512,1024]{1,0:T(8,128)S(1)} %copy-done, f32[512]{0:T(512)S(1)} %add_rsqrt_fusion), kind=kCustom, calls=%fused_computation.19 | custom fusion | flops 1048576 | bytes 4196354 | tf_op jit(solution)/shard_map/scatter | solution.py:34
  14.7 4.1 %reshape.106 = bf16[128,2,4,1024]{3,2,1,0:T(4,128)(2,1)} reshape(bf16[1024,1024]{1,0:T(8,128)(2,1)} %scatter_custom_fusion) | data formatting | bytes 4194304 | tf_op jit(solution)/shard_map/reshape | solution.py:36
  18.8 15.9 %all-to-all-start = ((bf16[128,2,4,1024]{3,2,1,0:T(4,128)(2,1)}), bf16[128,2,4,1024]{3,2,1,0:T(4,128)(2,1)}, u32[]{:S(2)}, u32[]{:S(2)}) async-start(bf16[128,2,4,1024]{3,2,1,0:T(4,128)(2,1)} %reshape.106), calls=%async_computation | async-start | bytes 4194304 | tf_op jit(solution)/shard_map/all_to_all | solution.py:41
  34.8 0.0 all-reduce.2.cloned.1.call-start
  34.8 1.7 fusion.12
  36.5 0.0 all-reduce.2.cloned.1.call-update
  36.5 268.0 %all-reduce.2.cloned.1.call-done = f32[256,1024]{1,0:T(8,128)} async-done(((f32[256,1024]{1,0:T(8,128)}), f32[256,1024]{1,0:T(8,128)}) %all-reduce.2.cloned.1.call-update) | async-done | bytes 1048592 | tf_op jit(solution)/shard_map/psum | solution.py:56
  304.5 1.4 multiply_reduce_fusion.1
  306.6 0.0 all-to-all-done
  306.6 2.3 slice_bitcast_fusion.1
  308.9 1.5 pad_maximum_fusion.1
  310.4 5.4 %all_to_all.10 = bf16[2,128,1,4,1024]{4,3,1,2,0:T(4,128)(2,1)S(1)} all-to-all(bf16[2,128,1,4,1024]{4,3,1,2,0:T(4,128)(2,1)S(1)} %pad_maximum_fusion.1), channel_id=1, replica_groups=mesh['dp'=128,'rep'=2] {'rep'}, dimensions={0} | all-to-all | bytes 4194304 | tf_op jit(solution)/shard_map/all_to_all | solution.py:38
  315.8 2.6 copy.10
  318.4 2.5 reshape_reshape.3
  320.9 0.0 copy-start.2
  321.0 0.5 fusion.6
  321.4 2.5 fusion.15
  323.9 0.6 broadcast_select_fusion
  324.5 0.6 convert_reduce_fusion
  326.5 0.0 copy-done.2
  326.5 0.1 remainder_bitcast_fusion
  326.7 4.4 %sort.17 = (s32[1024]{0:T(1024)}, s32[1024]{0:T(1024)S(1)}) sort(s32[1024]{0:T(1024)S(1)} %get-tuple-element.75, s32[1024]{0:T(1024)S(1)} %iota.25), dimensions={0}, to_apply=%region_5.6 | sort | flops 10240 | bytes 16384 | tf_op jit(solution)/shard_map/jit(argsort)/sort | solution.py:63
  331.0 2.3 gather_fusion
  333.3 2.1 gather_fusion.1
  335.4 1.1 fusion.21
  336.5 2.1 collective-permute-start
  338.6 7.7 %collective-permute-start.1 = (bf16[256,1024]{1,0:T(8,128)(2,1)}, bf16[256,1024]{1,0:T(8,128)(2,1)S(1)}, u32[]{:S(2)}, u32[]{:S(2)}) collective-permute-start(bf16[256,1024]{1,0:T(8,128)(2,1)} %get-tuple-element.73), channel_id=1, source_target_pairs={{1,0},{2,1},{3,2},{4,3},{5,4},{6,5},{7,6},{8,7},{9,8},{10,9},{11,1... | collective-permute-start | bytes 1572872 | tf_op jit(solution)/shard_map/ppermute | solution.py:13
  346.3 5.1 %collective-permute-done = bf16[256,1024]{1,0:T(8,128)(2,1)S(1)} collective-permute-done((bf16[256,1024]{1,0:T(8,128)(2,1)}, bf16[256,1024]{1,0:T(8,128)(2,1)S(1)}, u32[]{:S(2)}, u32[]{:S(2)}) %collective-permute-start) | collective-permute-done | bytes 524320 | tf_op jit(solution)/shard_map/ppermute | solution.py:13
  351.4 1.9 collective-permute-done.1
  353.2 1.9 pad_maximum_fusion
  355.1 13.6 %while.11 = (s32[]{:T(128)}, f32[2,512]{1,0:T(2,128)S(1)}, pred[1536]{0:T(1024)(128)(4,1)S(1)}, s32[2]{0:T(128)S(1)}, bf16[1024,1024]{1,0:T(8,128)(2,1)S(1)}, /*...) while((s32[]{:T(128)}, f32[2,512]{1,0:T(2,128)S(1)}, ...), condition=%wide.region_9.10_spmd.clone, body=%wide.region_7.9_spmd.clone.sunk | while | flops 1613758464 | bytes 4206743 | solution.py:86
  355.1 0.5 dynamic_slice.23
  357.3 0.5 iota_add_fusion.2
  357.9 4.0 %fusion.29 = f32[512]{0:T(512)S(1)} fusion(bf16[1536,1024]{1,0:T(8,128)(2,1)} %get-tuple-element.136, s32[512]{0:T(512)S(1)} %iota_add_fusion.2, pred[1536]{0:T(1024)(128)(4,1)S(1)} %get-tuple-element.133, bf16[1024,1024]{1,0:T(8,128)(2,1)S(1)} %get-tuple-element.135, s32[]{:T(128)S(6)} %select_n.90), kind=kOutput, calls=%fused_computation.7.clone.1 | convolution fusion | flops 1613757952 | bytes 4200452 | tf_op jit(solution)/shard_map/while/body/eval_jaxpr/dot_general | solution.py:78
  361.9 0.6 dynamic_slice.23
  364.1 0.5 iota_add_fusion.2
  364.7 4.0 %fusion.29 = f32[512]{0:T(512)S(1)} fusion(bf16[1536,1024]{1,0:T(8,128)(2,1)} %get-tuple-element.136, s32[512]{0:T(512)S(1)} %iota_add_fusion.2, pred[1536]{0:T(1024)(128)(4,1)S(1)} %get-tuple-element.133, bf16[1024,1024]{1,0:T(8,128)(2,1)S(1)} %get-tuple-element.135, s32[]{:T(128)S(6)} %select_n.90), kind=kOutput, calls=%fused_computation.7.clone.1 | convolution fusion | flops 1613757952 | bytes 4200452 | tf_op jit(solution)/shard_map/while/body/eval_jaxpr/dot_general | solution.py:78
  368.8 0.6 broadcast_select_fusion.1
  (22 shorter events, 0.2 us)
Async XLA Ops:
  7.2 1.8 copy-start.1
  9.0 1.6 copy-start
  18.8 287.7 %all-to-all-start = ((bf16[128,2,4,1024]{3,2,1,0:T(4,128)(2,1)}), bf16[128,2,4,1024]{3,2,1,0:T(4,128)(2,1)}, u32[]{:S(2)}, u32[]{:S(2)}) async-start(bf16[128,2,4,1024]{3,2,1,0:T(4,128)(2,1)} %reshape.106), calls=%async_computation | async-start | bytes 4194304 | tf_op jit(solution)/shard_map/all_to_all | solution.py:41
  34.8 269.8 %all-reduce.2.cloned.1.call-start = ((), (), s32[]{:S(2)}) async-start(), calls=%async_computation.2 | async-start | bytes 2097152 | tf_op jit(solution)/shard_map/psum | solution.py:56
  320.9 5.5 %copy-start.2 = (s32[1,2,256]{2,1,0:T(2,128)S(1)}, s32[1,2,256]{2,1,0:T(2,128)}, u32[]{:S(2)}) copy-start(s32[1,2,256]{2,1,0:T(2,128)} %param.7) | copy-start | bytes 6148
  336.5 14.9 %collective-permute-start = (bf16[256,1024]{1,0:T(8,128)(2,1)}, bf16[256,1024]{1,0:T(8,128)(2,1)S(1)}, u32[]{:S(2)}, u32[]{:S(2)}) collective-permute-start(bf16[256,1024]{1,0:T(8,128)(2,1)} %get-tuple-element.72), channel_id=1, source_target_pairs={{0,1},{1,2},{2,3},{3,4},{4,5},{5,6},{6,7},{7,8},{8,9},{9,10},{10,1... | collective-permute-start | bytes 1572872 | tf_op jit(solution)/shard_map/ppermute | solution.py:13
  338.6 14.7 %collective-permute-start.1 = (bf16[256,1024]{1,0:T(8,128)(2,1)}, bf16[256,1024]{1,0:T(8,128)(2,1)S(1)}, u32[]{:S(2)}, u32[]{:S(2)}) collective-permute-start(bf16[256,1024]{1,0:T(8,128)(2,1)} %get-tuple-element.73), channel_id=1, source_target_pairs={{1,0},{2,1},{3,2},{4,3},{5,4},{6,5},{7,6},{8,7},{9,8},{10,9},{11,1... | collective-permute-start | bytes 1572872 | tf_op jit(solution)/shard_map/ppermute | solution.py:13
Sparse Core Ops, SparseCore 0:
  41.0 263.4 all-reduce.1
